TPU v7x, 32 devices: a whole 2x2x4 slice. The times are simulated.
32 devices in a mesh: lat: 4 (over y, x), lon: 8 (over z, core).
Axes of the slice: x: 2, y: 2, z: 4, core: 2. Of those that a mesh axis runs over, the one named last changes fastest.
Arguments:
- wind_u: float32 [32, 32, 1024], P(None, 'lat', 'lon'), may hold values from -6 to 6
- wind_v: float32 [32, 32, 1024], P(None, 'lat', 'lon'), may hold values from -6 to 6
Outputs:
- modes: float32 [32, 2, 32, 1024], P(None, None, 'lat', 'lon')
- factor: float32 [32, 32], replicated
All inputs are finite; a program needn't handle non-finite values.
Results may differ from a plain program's by a relative error of at most 0.0003.
Values sent between devices are 32-bit elements; how exact they have to be, the bound alone decides.
A program may use at most 64 MiB of HBM per device.

v0:
```python
import math

import jax
import jax.numpy as jnp
from jax import lax
from jax.sharding import PartitionSpec as P


def extended(block, sides, width, periodic):
    for axis, dim in sides:
        count = lax.axis_size(axis)
        forward = [(i, i + 1) for i in range(count - 1)]
        if periodic:
            forward.append((count - 1, 0))
        backward = [(target, source) for source, target in forward]
        low = lax.ppermute(
            lax.slice_in_dim(block, block.shape[dim] - width, None, axis=dim), axis, forward
        )
        high = lax.ppermute(lax.slice_in_dim(block, 0, width, axis=dim), axis, backward)
        block = jnp.concatenate([low, block, high], axis=dim)
    return block


def upper_factor(gram):
    count = gram.shape[0]
    positions = jnp.arange(count)

    def column_step(k, state):
        rest, lower = state
        onehot = (positions == k).astype(jnp.float32)
        below = (positions >= k).astype(jnp.float32)
        pivot = jnp.sum(rest * onehot[:, None] * onehot[None, :])
        column = jnp.sum(rest * onehot[None, :], axis=1) * below / jnp.sqrt(pivot)
        lower = lower + column[:, None] * onehot[None, :]
        rest = rest - column[:, None] * column[None, :]
        return (rest, lower)

    start = (gram, jnp.zeros(gram.shape, jnp.float32))
    rest, lower = lax.fori_loop(0, count, column_step, start)
    return lower.T


def inverse_upper(upper):
    count = upper.shape[0]
    positions = jnp.arange(count)

    def row_step(i, result):
        k = count - 1 - i
        onehot = (positions == k).astype(jnp.float32)
        row_of = jnp.sum(upper * onehot[:, None], axis=0)
        diag = jnp.sum(row_of * onehot)
        off_diag = row_of * (1.0 - onehot)
        new_row = (onehot - jnp.sum(off_diag[:, None] * result, axis=0)) / diag
        return result + onehot[:, None] * new_row[None, :]

    return lax.fori_loop(0, count, row_step, jnp.zeros(upper.shape, jnp.float32))


def inner(left, right):
    return jnp.dot(left, right, precision=lax.Precision.HIGHEST, preferred_element_type=jnp.float32)


def merge_gram(gram_local):
    return lax.psum(gram_local, ("lat", "lon"))


def shards(wind_u, wind_v):
    snaps, lat_cells, lon_cells = wind_u.shape
    winds = jnp.stack((wind_u, wind_v))
    nlat = lat_cells * lax.axis_size("lat")
    nlon = lon_cells * lax.axis_size("lon")
    step = 2.0 * math.pi / nlon
    first_row = lax.axis_index("lat") * lat_cells
    row_index = (first_row + jnp.arange(-1, lat_cells + 1)).astype(jnp.float32)
    cosines = jnp.cos((row_index + 0.5 - nlat / 2) * step)
    northward = extended(winds, (("lat", 2),), 1, False)
    weighted = northward * cosines[None, None, :, None]
    lat_diff = weighted[:, :, 2:, :] - weighted[:, :, :-2, :]
    eastward = extended(winds, (("lon", 3),), 1, True)
    lon_diff = eastward[..., 2:] - eastward[..., :-2]
    scale = (0.5 / jnp.sqrt(cosines[1:-1]))[None, :, None]
    vorticity = (lon_diff[1] - lat_diff[0]) * scale
    divergence = (lon_diff[0] + lat_diff[1]) * scale
    block = jnp.stack([vorticity, divergence], axis=1).reshape(snaps, -1)
    total_rows = block.shape[1] * lax.axis_size("lat") * lax.axis_size("lon")
    first = upper_factor(merge_gram(inner(block, block.T)))
    solved = inner(inverse_upper(first).T, block)
    second = upper_factor(merge_gram(inner(solved, solved.T)))
    root = math.sqrt(total_rows)
    modes = inner(inverse_upper(second).T, solved) * root
    factor = inner(second, first) / root
    return (modes.reshape(snaps, 2, lat_cells, lon_cells), factor)


def solution(mesh):
    in_specs = (P(None, "lat", "lon"), P(None, "lat", "lon"))
    out_specs = (P(None, None, "lat", "lon"), P())
    return jax.shard_map(shards, mesh=mesh, in_specs=in_specs, out_specs=out_specs, check_vma=False)
```

profile of v0, /device:TPU:0, one launch (start us, length us, event | category | flops | bytes accessed | tf_op | source)
XLA Modules:
  0.0 297.6 jit_solution(4057111785696801256)
XLA Ops:
  0.6 1.0 copy_bitcast_fusion
  1.7 4.9 %collective-permute-start.2 = (f32[2,32,1,128]{3,1,2,0:T(8,128)S(1)}, f32[2,32,1,128]{3,1,2,0:T(8,128)S(1)}, u32[]{:S(2)}, u32[]{:S(2)}) collective-permute-start(f32[2,32,1,128]{3,1,2,0:T(8,128)S(1)} %get-tuple-element.460), channel_id=1, source_target_pairs={{0,8},{8,16},{16,24},{1,9},{9,17},{17,25},{2,10},{10,18},{18,26},{... | collective-permute-start | bytes 98312 | tf_op jit(solution)/shard_map/ppermute | solution.py:16
  6.5 1.3 collective-permute-start.3
  8.0 2.8 collective-permute-start
  10.9 4.9 %collective-permute-done = f32[2,32,8,1]{3,1,2,0:T(8,128)S(1)} collective-permute-done((f32[2,32,8,1]{3,1,2,0:T(8,128)S(1)}, f32[2,32,8,1]{3,1,2,0:T(8,128)S(1)}, u32[]{:S(2)}, u32[]{:S(2)}) %collective-permute-start) | collective-permute-done | bytes 2080 | tf_op jit(solution)/shard_map/ppermute | solution.py:19
  15.9 2.9 collective-permute-done.1
  19.9 39.7 %psum.14 = f32[32,32]{1,0:T(8,128)S(1)} all-reduce(f32[32,32]{1,0:T(8,128)S(1)} %convolution_bitcast_fusion), channel_id=1, replica_groups=mesh['lat'=4,'lon'=8] {'lat','lon'}, use_global_device_ids=true, to_apply=%region_0.0 | all-reduce | flops 1024 | bytes 8192 | tf_op jit(solution)/shard_map/psum | solution.py:64
  59.5 44.0 %while.64 = (s32[]{:T(128)}, f32[32,32]{1,0:T(8,128)S(1)}, f32[32,32]{1,0:T(8,128)S(1)}, s32[]{:T(128)}, s32[]{:T(128)}) while((s32[]{:T(128)}, f32[32,32]{1,0:T(8,128)S(1)}, f32[32,32]{1,0:T(8,128)S(1)}, s32[]{:T(128)}, s32[]{:T(128)}) %tuple.149), condition=%wide.region_4.0_spmd.clone.clone, body=%wide.region_1.0_spmd.clone.clone.sunk | while | flops 10370 | bytes 21471 | solution.py:39
  103.6 45.7 %while.62 = (s32[]{:T(128)}, f32[32,32]{1,0:T(8,128)S(1)}, f32[32,32]{1,0:T(8,128)S(1)}, s32[]{:T(128)}, s32[]{:T(128)}, /*index=5*/s32[]{:T(128)}) while((s32[]{:T(128)}, f32[32,32]{1,0:T(8,128)S(1)}, f32[32,32]{1,0:T(8,128)S(1)}, s32[]{:T(128)}, s32[]{:T(128)}, /*index=5*/s32[]{:T(128)}) %tuple.152), condition=%wide.region_9.0_spmd.clone, body=%wide.region_5.0_spmd.clone.sunk | while | flops 8515 | bytes 17904 | solution.py:56
  150.1 41.8 %psum.15 = f32[32,32]{1,0:T(8,128)S(1)} all-reduce(f32[32,32]{1,0:T(8,128)S(1)} %fusion.24), channel_id=1, replica_groups=mesh['lat'=4,'lon'=8] {'lat','lon'}, use_global_device_ids=true, to_apply=%region_10.0 | all-reduce | flops 1024 | bytes 8192 | tf_op jit(solution)/shard_map/psum | solution.py:64
  191.9 50.9 %while.65 = (s32[]{:T(128)}, f32[32,32]{1,0:T(8,128)S(1)}, f32[32,32]{1,0:T(8,128)S(1)}, s32[]{:T(128)}, s32[]{:T(128)}) while((s32[]{:T(128)}, f32[32,32]{1,0:T(8,128)S(1)}, f32[32,32]{1,0:T(8,128)S(1)}, s32[]{:T(128)}, s32[]{:T(128)}) %tuple.155), condition=%wide.region_14.0_spmd.clone.clone, body=%wide.region_11.0_spmd.clone.clone.sunk | while | flops 10370 | bytes 21471 | solution.py:39
  191.9 0.8 multiply_reduce_fusion.19
  193.5 0.8 multiply_reduce_fusion.19
  195.1 0.8 multiply_reduce_fusion.19
  196.7 0.8 multiply_reduce_fusion.19
  198.3 0.8 multiply_reduce_fusion.19
  199.9 0.8 multiply_reduce_fusion.19
  201.5 0.8 multiply_reduce_fusion.19
  203.0 0.8 multiply_reduce_fusion.19
  204.6 0.8 multiply_reduce_fusion.19
  206.2 0.8 multiply_reduce_fusion.19
  207.8 0.8 multiply_reduce_fusion.19
  209.4 0.8 multiply_reduce_fusion.19
  211.0 0.8 multiply_reduce_fusion.19
  212.6 0.8 multiply_reduce_fusion.19
  214.2 0.8 multiply_reduce_fusion.19
  215.8 0.8 multiply_reduce_fusion.19
  217.4 0.8 multiply_reduce_fusion.19
  219.0 0.8 multiply_reduce_fusion.19
  220.6 0.8 multiply_reduce_fusion.19
  222.2 0.8 multiply_reduce_fusion.19
  223.7 0.8 multiply_reduce_fusion.19
  225.3 0.8 multiply_reduce_fusion.19
  226.9 0.8 multiply_reduce_fusion.19
  228.5 0.8 multiply_reduce_fusion.19
  230.1 0.8 multiply_reduce_fusion.19
  231.7 0.8 multiply_reduce_fusion.19
  233.3 0.8 multiply_reduce_fusion.19
  234.9 0.8 multiply_reduce_fusion.19
  236.5 0.8 multiply_reduce_fusion.19
  238.1 0.8 multiply_reduce_fusion.19
  239.7 0.8 multiply_reduce_fusion.19
  241.3 0.8 multiply_reduce_fusion.19
  242.8 0.8 convolution_multiply_fusion.1
  243.7 52.7 %while.63 = (s32[]{:T(128)}, f32[32,32]{1,0:T(8,128)S(1)}, f32[32,32]{1,0:T(8,128)S(1)}, s32[]{:T(128)}, s32[]{:T(128)}, /*index=5*/s32[]{:T(128)}) while((s32[]{:T(128)}, f32[32,32]{1,0:T(8,128)S(1)}, f32[32,32]{1,0:T(8,128)S(1)}, s32[]{:T(128)}, s32[]{:T(128)}, /*index=5*/s32[]{:T(128)}) %tuple.158), condition=%wide.region_19.0_spmd.clone, body=%wide.region_15.0_spmd.clone.sunk | while | flops 8515 | bytes 17904 | solution.py:56
  244.6 0.7 subtract_divide_fusion.5
  246.3 0.7 subtract_divide_fusion.5
  296.9 0.8 copy.15
  (629 shorter events, 125.9 us)
Async XLA Ops:
  1.7 17.4 %collective-permute-start.2 = (f32[2,32,1,128]{3,1,2,0:T(8,128)S(1)}, f32[2,32,1,128]{3,1,2,0:T(8,128)S(1)}, u32[]{:S(2)}, u32[]{:S(2)}) collective-permute-start(f32[2,32,1,128]{3,1,2,0:T(8,128)S(1)} %get-tuple-element.460), channel_id=1, source_target_pairs={{0,8},{8,16},{16,24},{1,9},{9,17},{17,25},{2,10},{10,18},{18,26},{... | collective-permute-start | bytes 98312 | tf_op jit(solution)/shard_map/ppermute | solution.py:16
  6.5 12.5 %collective-permute-start.3 = (f32[2,32,1,128]{3,1,2,0:T(8,128)S(1)}, f32[2,32,1,128]{3,1,2,0:T(8,128)S(1)}, u32[]{:S(2)}, u32[]{:S(2)}) collective-permute-start(f32[2,32,1,128]{3,1,2,0:T(8,128)S(1)} %get-tuple-element.461), channel_id=1, source_target_pairs={{8,0},{16,8},{24,16},{9,1},{17,9},{25,17},{10,2},{18,10},{26,18},{... | collective-permute-start | bytes 98312 | tf_op jit(solution)/shard_map/ppermute | solution.py:19
  8.0 7.9 %collective-permute-start = (f32[2,32,8,1]{3,1,2,0:T(8,128)S(1)}, f32[2,32,8,1]{3,1,2,0:T(8,128)S(1)}, u32[]{:S(2)}, u32[]{:S(2)}) collective-permute-start(f32[2,32,8,1]{3,1,2,0:T(8,128)S(1)} %get-tuple-element.458), channel_id=1, source_target_pairs={{1,0},{2,1},{3,2},{4,3},{5,4},{6,5},{7,6},{0,7},{9,8},{10,9},{11,1... | collective-permute-start | bytes 6152 | tf_op jit(solution)/shard_map/ppermute | solution.py:19
  10.8 8.0 %collective-permute-start.1 = (f32[2,32,8,1]{3,1,2,0:T(8,128)S(1)}, f32[2,32,8,1]{3,1,2,0:T(8,128)S(1)}, u32[]{:S(2)}, u32[]{:S(2)}) collective-permute-start(f32[2,32,8,1]{3,1,2,0:T(8,128)S(1)} %get-tuple-element.459), channel_id=1, source_target_pairs={{0,1},{1,2},{2,3},{3,4},{4,5},{5,6},{6,7},{7,0},{8,9},{9,10},{10,1... | collective-permute-start | bytes 6152 | tf_op jit(solution)/shard_map/ppermute | solution.py:16
where the time goes:
time: 299 us; the launch traced here: 298 us
  other arithmetic  150 us (50%)
  blocking collectives  81.5 us (27%)
  loops' own time  44.5 us (15%)
  starting transfers between devices  8.98 us (3%)
  waiting for transfers between devices  7.88 us (3%)
    psum x2, blocking collectives, merge_gram(): return lax.psum(gram_local, ('lat', 'lon'))  81.5 us
    reduce_sum x64, other arithmetic, column_step(): pivot = jnp.sum(rest * onehot[:, None] * onehot[None, :])  45.7 us
    another operation x2, loops' own time, upper_factor(): rest, lower = lax.fori_loop(0, count, column_step, start)  43.8 us
    reduce_sum x64, other arithmetic, row_step(): diag = jnp.sum(row_of * onehot)  40.9 us
    div x64, other arithmetic, row_step(): new_row = (onehot - jnp.sum(off_diag[:, None] * result, axis=0)) / diag  40.2 us
  transfers between devices with their start and end apart: 4, of which 2 were waited for; matrix products, arithmetic and copies ran while one was open for 0% of the time, Pallas kernels for 0%

commit v1 on v0

v1 whole, which is shorter than its diff:
```python
import functools
import math

import jax
import jax.numpy as jnp
from jax import lax
from jax.experimental import pallas as pl
from jax.experimental.pallas import tpu as pltpu
from jax.sharding import PartitionSpec as P

MESH = pl.DeviceIdType.MESH
LANES = 128
SUBS = 8
BLOCK = 8


def iota(shape, dim):
    return lax.broadcasted_iota(jnp.int32, shape, dim)


def dot(left, right, dims):
    return lax.dot_general(
        left,
        right,
        (dims, ((), ())),
        precision=lax.Precision.HIGHEST,
        preferred_element_type=jnp.float32,
    )


def roll(tile, shift):
    shift = shift % LANES
    return tile if shift == 0 else pltpu.roll(tile, shift, 1)


def spread(tile):
    return jnp.broadcast_to(tile, (SUBS, LANES))


def pack_gram(gram):
    n = gram.shape[0]
    return jnp.concatenate([gram[g * SUBS : (g + 1) * SUBS] for g in range(n // SUBS)], axis=1)


def factorize(packed, n):
    groups = n // SUBS
    lane = iota((SUBS, LANES), 1)
    sub = iota((SUBS, LANES), 0)
    rows = []
    for g in range(groups):
        unit = jnp.where(lane == sub + g * SUBS, 1.0, 0.0)
        rows.append(jnp.where(lane < n, unit, roll(packed, n - g * n)))
    pivots = [None] * groups
    for start in range(0, n, BLOCK):
        r = start // SUBS
        columns = [
            [spread(rows[g][:, n + k : n + k + 1]) if g >= r else None for g in range(groups)]
            for k in range(start, start + BLOCK)
        ]
        for step in range(BLOCK):
            k = start + step
            s = k % SUBS
            pivot = spread(columns[step][r][s : s + 1, :])
            pivots[r] = pivot if s == 0 else jnp.where(sub == s, pivot, pivots[r])
            inverse = 1.0 / pivot
            pivot_row = spread(rows[r][s : s + 1, :]) * inverse
            heads = [
                spread(columns[later][r][s : s + 1, :]) * inverse for later in range(step + 1, BLOCK)
            ]
            for g in range(r, groups):
                factor = columns[step][g]
                if g == r:
                    if s == SUBS - 1:
                        continue
                    factor = jnp.where(sub > s, factor, 0.0)
                rows[g] = rows[g] - factor * pivot_row
                for later in range(step + 1, BLOCK):
                    columns[later][g] = columns[later][g] - factor * heads[later - step - 1]
    out = []
    for g in range(groups):
        scaled = rows[g] * (1.0 / jnp.sqrt(pivots[g]))
        keep = (lane < n) | (lane - n >= sub + g * SUBS)
        out.append(jnp.where(keep, scaled, 0.0))
    return jnp.concatenate(out, axis=0)


def kernel(
    sizes,
    u_ref,
    v_ref,
    modes_ref,
    factor_ref,
    x_ref,
    lat_out,
    lat_in,
    lon_out,
    lon_in,
    first_buf,
    second_buf,
    lat_send,
    lat_recv,
    lon_send,
    lon_recv,
    first_send,
    first_recv,
    second_send,
    second_recv,
):
    lat_size, lon_size, cores = sizes
    snaps, cells, width = u_ref.shape
    depth = lon_size // cores
    members = lat_size * cores
    lat = lax.axis_index("lat")
    lon = lax.axis_index("lon")
    z = lon // cores
    core = lon % cores
    mine = lat * cores + core
    lat_up = (lat + 1) % lat_size
    lat_down = (lat + lat_size - 1) % lat_size
    east = (lon + 1) % lon_size
    west = (lon + lon_size - 1) % lon_size

    def member(d):
        other = (mine + d) % members
        return other, (other // cores, z * cores + other % cores)

    def plane(d):
        other = (z + d) % depth
        return other, (lat, other * cores + core)

    barrier = pltpu.get_barrier_semaphore()
    peers = [member(d)[1] for d in range(1, members)] + [plane(d)[1] for d in range(1, depth)]
    peers += [(lat, east), (lat, west)]
    for peer in peers:
        pl.semaphore_signal(barrier, inc=1, device_id=peer, device_id_type=MESH)

    lane = iota((SUBS, LANES), 1)
    fields = (u_ref, v_ref)
    parts = snaps // SUBS
    winds = [[ref[:, i, :] for i in range(cells)] for ref in fields]
    for f in range(2):
        lat_out[0, f] = winds[f][cells - 1]
        lat_out[1, f] = winds[f][0]
    edge = jnp.zeros((SUBS, LANES), jnp.float32)
    for f in range(2):
        for i in range(cells):
            for t in range(parts):
                q = (f * cells + i) * parts + t
                tile = winds[f][i][t * SUBS : (t + 1) * SUBS]
                edge = jnp.where(lane // 2 == q, roll(tile, 2 * q + 1), edge)
    lon_out[...] = edge

    pl.semaphore_wait(barrier, len(peers))

    copies = []
    for way, target in ((0, lat_up), (1, lat_down)):
        copies.append(
            pltpu.make_async_remote_copy(
                src_ref=lat_out.at[way],
                dst_ref=lat_in.at[way],
                send_sem=lat_send.at[way],
                recv_sem=lat_recv.at[way],
                device_id=(target, lon),
                device_id_type=MESH,
            )
        )
    for way, target in ((0, east), (1, west)):
        copies.append(
            pltpu.make_async_remote_copy(
                src_ref=lon_out,
                dst_ref=lon_in.at[way],
                send_sem=lon_send.at[way],
                recv_sem=lon_recv.at[way],
                device_id=(lat, target),
                device_id_type=MESH,
            )
        )
    for copy in copies:
        copy.start()

    nlat = lat_size * cells
    step = 2.0 * math.pi / (lon_size * width)
    row_index = lat * cells - 1 + iota((2 * SUBS, LANES), 0)
    cosines = jnp.cos((row_index.astype(jnp.float32) + 0.5 - nlat / 2) * step)
    weights = jnp.where((row_index >= 0) & (row_index < nlat), cosines, 0.0)
    scales = 0.5 / jnp.sqrt(cosines)

    def weight(i):
        return weights[i + 1 : i + 2, :]

    def scale(i):
        return scales[i + 1 : i + 2, :]

    wide = iota((snaps, LANES), 1)

    def lon_inner(tile):
        right = jnp.where(wide == LANES - 1, 0.0, pltpu.roll(tile, LANES - 1, 1))
        return right - jnp.where(wide == 0, 0.0, pltpu.roll(tile, 1, 1))

    def lat_inner(f, i):
        high = weight(i + 1) * winds[f][i + 1] if i + 1 < cells else 0.0
        low = weight(i - 1) * winds[f][i - 1] if i > 0 else 0.0
        return high - low

    for i in range(cells):
        x_ref[i] = lon_inner(winds[1][i]) - lat_inner(0, i)
        x_ref[cells + i] = lon_inner(winds[0][i]) + lat_inner(1, i)

    for copy in copies:
        copy.wait_recv()

    ends = jnp.where(lane % 2 == 1, roll(lon_in[0], 1), roll(lon_in[1], LANES - 1))
    sign = jnp.where(lane == LANES - 1, 1.0, jnp.where(lane == 0, -1.0, 0.0))

    def lon_edge(f, i):
        pieces = []
        for t in range(parts):
            q = (f * cells + i) * parts + t
            pieces.append(sign * roll(ends, -(2 * q + 1)))
        return jnp.concatenate(pieces, axis=0)

    def lat_edge(f, i):
        total = 0.0
        if i == cells - 1:
            total = total + weight(cells) * lat_in[1, f]
        if i == 0:
            total = total - weight(-1) * lat_in[0, f]
        return total

    columns = []
    for i in range(cells):
        columns.append((x_ref[i] + lon_edge(1, i) - lat_edge(0, i)) * scale(i))
    for i in range(cells):
        columns.append((x_ref[cells + i] + lon_edge(0, i) + lat_edge(1, i)) * scale(i))
    block = jnp.concatenate(columns, axis=1)

    pending = []

    def exchange(buf, slot, count, peer_of, send, recv, at, value):
        buf[at, slot] = value
        for d in range(1, count):
            other, peer = peer_of(d)
            copy = pltpu.make_async_remote_copy(
                src_ref=buf.at[at, slot],
                dst_ref=buf.at[at, slot],
                send_sem=send.at[at, d - 1],
                recv_sem=recv.at[at, slot],
                device_id=peer,
                device_id_type=MESH,
            )
            copy.start()
            pending.append(copy)
        for d in range(1, count):
            other, peer = peer_of(d)
            pltpu.make_async_remote_copy(
                src_ref=buf.at[at, other],
                dst_ref=buf.at[at, other],
                send_sem=send.at[at, d - 1],
                recv_sem=recv.at[at, other],
                device_id=peer,
                device_id_type=MESH,
            ).wait_recv()
        total = buf[at, 0]
        for index in range(1, count):
            total = total + buf[at, index]
        return total

    def merged(value, at):
        value = exchange(first_buf, mine, members, member, first_send, first_recv, at, value)
        return exchange(second_buf, z, depth, plane, second_send, second_recv, at, value)

    root = math.sqrt(2 * nlat * lon_size * width)
    gram = dot(block, block, ((1,), (1,)))
    first = factorize(merged(pack_gram(gram), 0), snaps)
    solved = dot(first[:, :snaps], block, ((1,), (0,)))
    gram = dot(solved, solved, ((1,), (1,)))
    second = factorize(merged(pack_gram(gram), 1), snaps)
    modes = dot(second[:, :snaps] * root, solved, ((1,), (0,)))
    for f in range(2):
        for i in range(cells):
            at = (f * cells + i) * width
            modes_ref[:, f, i, :] = modes[:, at : at + width]
    upper = [pltpu.roll(m, LANES - snaps, 1)[:, :snaps] for m in (second, first)]
    factor_ref[...] = dot(upper[0], upper[1], ((1,), (0,))) / root

    for copy in copies + pending:
        copy.wait_send()


def shards(sizes, wind_u, wind_v):
    snaps, cells, width = wind_u.shape
    lat_size, lon_size, cores = sizes
    members, depth = lat_size * cores, lon_size // cores
    f32 = jnp.float32
    dma = pltpu.SemaphoreType.DMA
    vmem = pl.BlockSpec(memory_space=pltpu.VMEM)
    return pl.pallas_call(
        functools.partial(kernel, sizes),
        out_shape=(
            jax.ShapeDtypeStruct((snaps, 2, cells, width), f32),
            jax.ShapeDtypeStruct((snaps, snaps), f32),
        ),
        in_specs=[vmem, vmem],
        out_specs=(vmem, vmem),
        scratch_shapes=[
            pltpu.VMEM((2 * cells, snaps, width), f32),
            pltpu.VMEM((2, 2, snaps, width), f32),
            pltpu.VMEM((2, 2, snaps, width), f32),
            pltpu.VMEM((SUBS, LANES), f32),
            pltpu.VMEM((2, SUBS, LANES), f32),
            pltpu.VMEM((2, members, SUBS, LANES), f32),
            pltpu.VMEM((2, depth, SUBS, LANES), f32),
            dma((2,)),
            dma((2,)),
            dma((2,)),
            dma((2,)),
            dma((2, members)),
            dma((2, members)),
            dma((2, depth)),
            dma((2, depth)),
        ],
        compiler_params=pltpu.CompilerParams(collective_id=0, has_side_effects=True),
    )(wind_u, wind_v)


def solution(mesh):
    lat_size, lon_size = mesh.shape["lat"], mesh.shape["lon"]
    sizes = (lat_size, lon_size, 2 if lon_size % 2 == 0 else 1)
    in_specs = (P(None, "lat", "lon"), P(None, "lat", "lon"))
    out_specs = (P(None, None, "lat", "lon"), P())
    return jax.shard_map(
        functools.partial(shards, sizes),
        mesh=mesh,
        in_specs=in_specs,
        out_specs=out_specs,
        check_vma=False,
    )
```

time: 299 us -> 32.2 us (0.11)
  other arithmetic: 150 us -> 0 us
  blocking collectives: 81.5 us -> 0 us
  loops' own time: 44.5 us -> 0 us
  Pallas kernels: 0 us -> 29.2 us
  starting transfers between devices: 8.98 us -> 0 us
  waiting for transfers between devices: 7.88 us -> 0 us
    reduce_sum x256 -> x0, other arithmetic: 98.3 us -> none  [the longest x64 45.7 us: column_step(): pivot = jnp.sum(rest * onehot[:, None] * onehot[None, :])]
    psum x2 -> x0, blocking collectives: 81.5 us -> none  [merge_gram(): return lax.psum(gram_local, ('lat', 'lon'))]
    another operation x4 -> x0, loops' own time: 44.5 us -> none  [the longest x2 43.8 us: upper_factor(): rest, lower = lax.fori_loop(0, count, column_step, start)]
    div x129 -> x0, other arithmetic: 40.6 us -> none  [the longest x64 40.2 us: row_step(): new_row = (onehot - jnp.sum(off_diag[:, None] * result, axis=0)) / diag]
    pallas_call x0 -> x1, Pallas kernels: none -> 29.2 us  [shards(): pl.pallas_call(functools.partial(kernel, sizes), out_shape=(jax.ShapeDtyp...]
    add x128 -> x0, other arithmetic: 9.7 us -> none  [the longest x64 4.88 us: column_step(): lower = lower + column[:, None] * onehot[None, :]]
    ppermute x4 -> x0, starting transfers between devices: 8.98 us -> none  [the longest x2 4.88 us: extended(): lax.ppermute(lax.slice_in_dim(block, block.shape[dim] - width, None, axis...]
    ppermute x4 -> x0, waiting for transfers between devices: 7.88 us -> none  [the longest x2 4.93 us: extended(): lax.ppermute(lax.slice_in_dim(block, 0, width, axis=dim), axis, backward)]
  transfers between devices with their start and end apart: 4 -> 0, of which waited for: 2 -> 0; matrix products, arithmetic and copies ran while one was open for 0% -> 0% of each run, Pallas kernels for 0% -> 0%
where the time goes in v1:
time: 32.2 us; the launch traced here: 32.1 us
  Pallas kernels  29.2 us (91%)
  local copies, waits for them, and re-layouts  2.28 us (7%)
  between operations  0.65 us (2%)
    pallas_call x1, Pallas kernels, shards(): pl.pallas_call(functools.partial(kernel, sizes), out_shape=(jax.ShapeDtyp...  29.2 us
    unnamed x4, local copies, waits for them, and re-layouts  2.28 us

profile of v1, /device:TPU:0, one launch (start us, length us, event | category | flops | bytes accessed | tf_op | source)
XLA Modules:
  0.0 32.1 jit_solution(9778071895962906061)
XLA Ops:
  0.6 29.2 %shard_map.41 = (f32[32,2,8,128]{3,2,1,0:T(8,128)}, f32[32,32]{1,0:T(8,128)}) custom-call(f32[32,8,128]{2,1,0:T(8,128)} %u_ref.1, f32[32,8,128]{2,1,0:T(8,128)} %v_ref.1), custom_call_target="tpu_custom_call" | custom-call | tf_op jit(solution)/shard_map/pallas_call | solution.py:297
  29.8 0.0 copy-start
  29.8 1.7 %copy.6 = f32[32,2,8,128]{3,2,1,0:T(8,128)} copy(f32[32,2,8,128]{3,2,1,0:T(8,128)} %get-tuple-element.4) | data formatting | bytes 524288
  31.5 0.0 copy-done
  31.5 0.6 %copy.7 = f32[32,32]{1,0:T(8,128)} copy(f32[32,32]{1,0:T(8,128)S(1)} %copy-done) | data formatting | bytes 8192
Async XLA Ops:
  29.8 1.7 %copy-start = (f32[32,32]{1,0:T(8,128)S(1)}, f32[32,32]{1,0:T(8,128)}, u32[]{:S(2)}) copy-start(f32[32,32]{1,0:T(8,128)} %get-tuple-element.5) | copy-start | bytes 12292

commit v2 on v1

--- a/solution.py
+++ b/solution.py
@@ -86,58 +86,69 @@
 
 def kernel(
     sizes,
-    u_ref,
-    v_ref,
-    modes_ref,
-    factor_ref,
+    u_hbm,
+    v_hbm,
+    solved_ref,
+    first_ref,
+    second_ref,
+    wind_ref,
     x_ref,
     lat_out,
     lat_in,
     lon_out,
     lon_in,
-    first_buf,
-    second_buf,
+    pair_buf,
+    chip_buf,
     lat_send,
     lat_recv,
     lon_send,
     lon_recv,
-    first_send,
-    first_recv,
-    second_send,
-    second_recv,
+    pair_send,
+    pair_recv,
+    chip_send,
+    chip_recv,
+    local_sem,
 ):
     lat_size, lon_size, cores = sizes
-    snaps, cells, width = u_ref.shape
+    _, snaps, cells, width = wind_ref.shape
     depth = lon_size // cores
-    members = lat_size * cores
+    chips = lat_size * depth
     lat = lax.axis_index("lat")
     lon = lax.axis_index("lon")
     z = lon // cores
     core = lon % cores
-    mine = lat * cores + core
+    mine = lat * depth + z
     lat_up = (lat + 1) % lat_size
     lat_down = (lat + lat_size - 1) % lat_size
     east = (lon + 1) % lon_size
     west = (lon + lon_size - 1) % lon_size
 
-    def member(d):
-        other = (mine + d) % members
-        return other, (other // cores, z * cores + other % cores)
-
-    def plane(d):
-        other = (z + d) % depth
-        return other, (lat, other * cores + core)
+    def twin(d):
+        other = (core + d) % cores
+        return other, (lat, z * cores + other)
+
+    def chip(d):
+        other = (mine + d) % chips
+        return other, (other // depth, (other % depth) * cores + core)
 
     barrier = pltpu.get_barrier_semaphore()
-    peers = [member(d)[1] for d in range(1, members)] + [plane(d)[1] for d in range(1, depth)]
+    peers = [chip(d)[1] for d in range(1, chips)] + [twin(d)[1] for d in range(1, cores)]
     peers += [(lat, east), (lat, west)]
     for peer in peers:
         pl.semaphore_signal(barrier, inc=1, device_id=peer, device_id_type=MESH)
 
+    loads = [
+        pltpu.make_async_copy(hbm, wind_ref.at[f], local_sem.at[f])
+        for f, hbm in enumerate((u_hbm, v_hbm))
+    ]
+    for load in loads:
+        load.start()
+    for load in loads:
+        load.wait()
+
     lane = iota((SUBS, LANES), 1)
-    fields = (u_ref, v_ref)
     parts = snaps // SUBS
-    winds = [[ref[:, i, :] for i in range(cells)] for ref in fields]
+    winds = [[wind_ref[f, :, i, :] for i in range(cells)] for f in range(2)]
     for f in range(2):
         lat_out[0, f] = winds[f][cells - 1]
         lat_out[1, f] = winds[f][0]
@@ -175,8 +186,13 @@
                 device_id_type=MESH,
             )
         )
-    for copy in copies:
-        copy.start()
+    for at, copy in enumerate(copies):
+        if at == 0:
+            pl.when(lat < lat_size - 1)(copy.start)
+        elif at == 1:
+            pl.when(lat > 0)(copy.start)
+        else:
+            copy.start()
 
     nlat = lat_size * cells
     step = 2.0 * math.pi / (lon_size * width)
@@ -206,8 +222,13 @@
         x_ref[i] = lon_inner(winds[1][i]) - lat_inner(0, i)
         x_ref[cells + i] = lon_inner(winds[0][i]) + lat_inner(1, i)
 
-    for copy in copies:
-        copy.wait_recv()
+    for at, copy in enumerate(copies):
+        if at == 0:
+            pl.when(lat > 0)(copy.wait_recv)
+        elif at == 1:
+            pl.when(lat < lat_size - 1)(copy.wait_recv)
+        else:
+            copy.wait_recv()
 
     ends = jnp.where(lane % 2 == 1, roll(lon_in[0], 1), roll(lon_in[1], LANES - 1))
     sign = jnp.where(lane == LANES - 1, 1.0, jnp.where(lane == 0, -1.0, 0.0))
@@ -266,16 +287,30 @@
         return total
 
     def merged(value, at):
-        value = exchange(first_buf, mine, members, member, first_send, first_recv, at, value)
-        return exchange(second_buf, z, depth, plane, second_send, second_recv, at, value)
-
-    root = math.sqrt(2 * nlat * lon_size * width)
+        value = exchange(pair_buf, core, cores, twin, pair_send, pair_recv, at, value)
+        return exchange(chip_buf, mine, chips, chip, chip_send, chip_recv, at, value)
+
     gram = dot(block, block, ((1,), (1,)))
     first = factorize(merged(pack_gram(gram), 0), snaps)
+    first_ref[...] = first
     solved = dot(first[:, :snaps], block, ((1,), (0,)))
+    solved_ref[...] = solved
     gram = dot(solved, solved, ((1,), (1,)))
-    second = factorize(merged(pack_gram(gram), 1), snaps)
-    modes = dot(second[:, :snaps] * root, solved, ((1,), (0,)))
+    second_ref[...] = factorize(merged(pack_gram(gram), 1), snaps)
+
+    for at, copy in enumerate(copies + pending):
+        if at == 0:
+            pl.when(lat < lat_size - 1)(copy.wait_send)
+        elif at == 1:
+            pl.when(lat > 0)(copy.wait_send)
+        else:
+            copy.wait_send()
+
+
+def finish(root, solved_ref, first_ref, second_ref, modes_ref, factor_ref):
+    snaps, _, cells, width = modes_ref.shape
+    first, second = first_ref[...], second_ref[...]
+    modes = dot(second[:, :snaps] * root, solved_ref[...], ((1,), (0,)))
     for f in range(2):
         for i in range(cells):
             at = (f * cells + i) * width
@@ -283,44 +318,55 @@
     upper = [pltpu.roll(m, LANES - snaps, 1)[:, :snaps] for m in (second, first)]
     factor_ref[...] = dot(upper[0], upper[1], ((1,), (0,))) / root
 
-    for copy in copies + pending:
-        copy.wait_send()
-
 
 def shards(sizes, wind_u, wind_v):
     snaps, cells, width = wind_u.shape
     lat_size, lon_size, cores = sizes
-    members, depth = lat_size * cores, lon_size // cores
+    chips = lat_size * lon_size // cores
     f32 = jnp.float32
     dma = pltpu.SemaphoreType.DMA
     vmem = pl.BlockSpec(memory_space=pltpu.VMEM)
-    return pl.pallas_call(
+    anywhere = pl.BlockSpec(memory_space=pl.ANY)
+    held = pl.pallas_call(
         functools.partial(kernel, sizes),
         out_shape=(
-            jax.ShapeDtypeStruct((snaps, 2, cells, width), f32),
-            jax.ShapeDtypeStruct((snaps, snaps), f32),
+            jax.ShapeDtypeStruct((snaps, 2 * cells * width), f32),
+            jax.ShapeDtypeStruct((snaps, LANES), f32),
+            jax.ShapeDtypeStruct((snaps, LANES), f32),
         ),
-        in_specs=[vmem, vmem],
-        out_specs=(vmem, vmem),
+        in_specs=[anywhere, anywhere],
+        out_specs=(vmem, vmem, vmem),
         scratch_shapes=[
+            pltpu.VMEM((2, snaps, cells, width), f32),
             pltpu.VMEM((2 * cells, snaps, width), f32),
             pltpu.VMEM((2, 2, snaps, width), f32),
             pltpu.VMEM((2, 2, snaps, width), f32),
             pltpu.VMEM((SUBS, LANES), f32),
             pltpu.VMEM((2, SUBS, LANES), f32),
-            pltpu.VMEM((2, members, SUBS, LANES), f32),
-            pltpu.VMEM((2, depth, SUBS, LANES), f32),
-            dma((2,)),
-            dma((2,)),
-            dma((2,)),
-            dma((2,)),
-            dma((2, members)),
-            dma((2, members)),
-            dma((2, depth)),
-            dma((2, depth)),
+            pltpu.VMEM((2, cores, SUBS, LANES), f32),
+            pltpu.VMEM((2, chips, SUBS, LANES), f32),
+            dma((2,)),
+            dma((2,)),
+            dma((2,)),
+            dma((2,)),
+            dma((2, cores)),
+            dma((2, cores)),
+            dma((2, chips)),
+            dma((2, chips)),
+            dma((2,)),
         ],
         compiler_params=pltpu.CompilerParams(collective_id=0, has_side_effects=True),
     )(wind_u, wind_v)
+    root = math.sqrt(2 * lat_size * cells * lon_size * width)
+    return pl.pallas_call(
+        functools.partial(finish, root),
+        out_shape=(
+            jax.ShapeDtypeStruct((snaps, 2, cells, width), f32),
+            jax.ShapeDtypeStruct((snaps, snaps), f32),
+        ),
+        in_specs=[vmem, vmem, vmem],
+        out_specs=(vmem, vmem),
+    )(*held)
 
 
 def solution(mesh):

time: 32.2 us -> 28 us (0.87)
  local copies, waits for them, and re-layouts: 2.28 us -> 0 us
  Pallas kernels: 29.2 us -> 27.2 us
    pallas_call x1, Pallas kernels: 29.2 us -> 25.1 us  [shards(): pl.pallas_call(functools.partial(kernel, sizes), out_shape=(jax.ShapeDtyp...]
    unnamed x4 -> x0, local copies, waits for them, and re-layouts: 2.28 us -> none
    pallas_call x0 -> x1, Pallas kernels: none -> 2.08 us  [shards(): pl.pallas_call(functools.partial(finish, root), out_shape=(jax.ShapeDtype...]
where the time goes in v2:
time: 28 us; the launch traced here: 27.8 us
  Pallas kernels  27.2 us (97%)
  between operations  0.64 us (2%)
    pallas_call x1, Pallas kernels, shards(): pl.pallas_call(functools.partial(kernel, sizes), out_shape=(jax.ShapeDtyp...  25.1 us
    pallas_call x1, Pallas kernels, shards(): pl.pallas_call(functools.partial(finish, root), out_shape=(jax.ShapeDtype...  2.08 us

profile of v2, /device:TPU:0, one launch (start us, length us, event | category | flops | bytes accessed | tf_op | source)
XLA Modules:
  0.0 27.8 jit_solution(1968391507874863227)
XLA Ops:
  0.6 25.1 %shard_map.41 = (f32[32,2048]{1,0:T(8,128)}, f32[32,128]{1,0:T(8,128)}, f32[32,128]{1,0:T(8,128)}) custom-call(f32[32,8,128]{2,1,0:T(8,128)} %u_hbm.1, f32[32,8,128]{2,1,0:T(8,128)} %v_hbm.1), custom_call_target="tpu_custom_call" | custom-call | tf_op jit(solution)/shard_map/pallas_call | solution.py:330
  25.8 2.1 %shard_map.42 = (f32[32,2,8,128]{3,2,1,0:T(8,128)}, f32[32,32]{1,0:T(8,128)}) custom-call(f32[32,2048]{1,0:T(8,128)} %get-tuple-element.5.solved_ref, f32[32,128]{1,0:T(8,128)} %get-tuple-element.6.first_ref, f32[32,128]{1,0:T(8,128)} %get-tuple-element.7.second_ref), custom_call_target="tpu_custom_call" | custom-call | tf_op jit(solution)/shard_map/pallas_call | solution.py:361

commit v3 on v2

--- a/solution.py
+++ b/solution.py
@@ -12,6 +12,7 @@
 LANES = 128
 SUBS = 8
 BLOCK = 8
+VMEM_BYTES = 8 * 1024 * 1024
 
 
 def iota(shape, dim):
@@ -107,6 +108,7 @@
     pair_recv,
     chip_send,
     chip_recv,
+    relay_sem,
     local_sem,
 ):
     lat_size, lon_size, cores = sizes
@@ -132,8 +134,17 @@
         return other, (other // depth, (other % depth) * cores + core)
 
     barrier = pltpu.get_barrier_semaphore()
-    peers = [chip(d)[1] for d in range(1, chips)] + [twin(d)[1] for d in range(1, cores)]
-    peers += [(lat, east), (lat, west)]
+    def along(d):
+        return [(lat, (z + depth + s) % depth * cores + core) for s in (d, -d)]
+
+    strides = relay_strides(depth)
+    peers = [
+        ((lat + a) % lat_size, z * cores + (core + b) % cores)
+        for a in range(lat_size)
+        for b in range(cores)
+        if a or b
+    ]
+    peers += [(lat, east), (lat, west)] + (along(1) if depth > 1 else [])
     for peer in peers:
         pl.semaphore_signal(barrier, inc=1, device_id=peer, device_id_type=MESH)
 
@@ -194,6 +205,13 @@
         else:
             copy.start()
 
+    def relay(at):
+        for peer in along(strides[at]):
+            pl.semaphore_signal(relay_sem.at[at], inc=1, device_id=peer, device_id_type=MESH)
+
+    if strides:
+        relay(0)
+
     nlat = lat_size * cells
     step = 2.0 * math.pi / (lon_size * width)
     row_index = lat * cells - 1 + iota((2 * SUBS, LANES), 0)
@@ -221,6 +239,10 @@
     for i in range(cells):
         x_ref[i] = lon_inner(winds[1][i]) - lat_inner(0, i)
         x_ref[cells + i] = lon_inner(winds[0][i]) + lat_inner(1, i)
+
+    for at in range(1, len(strides)):
+        pl.semaphore_wait(relay_sem.at[at - 1], 2)
+        relay(at)
 
     for at, copy in enumerate(copies):
         if at == 0:
@@ -288,14 +310,16 @@
 
     def merged(value, at):
         value = exchange(pair_buf, core, cores, twin, pair_send, pair_recv, at, value)
+        if at == 0 and strides:
+            pl.semaphore_wait(relay_sem.at[len(strides) - 1], 2)
         return exchange(chip_buf, mine, chips, chip, chip_send, chip_recv, at, value)
 
     gram = dot(block, block, ((1,), (1,)))
     first = factorize(merged(pack_gram(gram), 0), snaps)
+    solved = dot(first[:, :snaps], block, ((1,), (0,)))
+    gram = dot(solved, solved, ((1,), (1,)))
+    solved_ref[...] = solved
     first_ref[...] = first
-    solved = dot(first[:, :snaps], block, ((1,), (0,)))
-    solved_ref[...] = solved
-    gram = dot(solved, solved, ((1,), (1,)))
     second_ref[...] = factorize(merged(pack_gram(gram), 1), snaps)
 
     for at, copy in enumerate(copies + pending):
@@ -319,6 +343,14 @@
     factor_ref[...] = dot(upper[0], upper[1], ((1,), (0,))) / root
 
 
+def relay_strides(depth):
+    strides, reach = [], 0
+    while reach < depth // 2:
+        strides.append(max(reach, 1))
+        reach += strides[-1]
+    return strides
+
+
 def shards(sizes, wind_u, wind_v):
     snaps, cells, width = wind_u.shape
     lat_size, lon_size, cores = sizes
@@ -326,15 +358,15 @@
     f32 = jnp.float32
     dma = pltpu.SemaphoreType.DMA
     vmem = pl.BlockSpec(memory_space=pltpu.VMEM)
-    anywhere = pl.BlockSpec(memory_space=pl.ANY)
+    hbm = pl.BlockSpec(memory_space=pltpu.HBM)
     held = pl.pallas_call(
         functools.partial(kernel, sizes),
         out_shape=(
-            jax.ShapeDtypeStruct((snaps, 2 * cells * width), f32),
-            jax.ShapeDtypeStruct((snaps, LANES), f32),
-            jax.ShapeDtypeStruct((snaps, LANES), f32),
+            pltpu.VMEM((snaps, 2 * cells * width), f32),
+            pltpu.VMEM((snaps, LANES), f32),
+            pltpu.VMEM((snaps, LANES), f32),
         ),
-        in_specs=[anywhere, anywhere],
+        in_specs=[hbm, hbm],
         out_specs=(vmem, vmem, vmem),
         scratch_shapes=[
             pltpu.VMEM((2, snaps, cells, width), f32),
@@ -353,10 +385,13 @@
             dma((2, cores)),
             dma((2, chips)),
             dma((2, chips)),
+            pltpu.SemaphoreType.REGULAR((max(len(relay_strides(lon_size // cores)), 1),)),
             dma((2,)),
         ],
-        compiler_params=pltpu.CompilerParams(collective_id=0, has_side_effects=True),
-    )(wind_u, wind_v)
+        compiler_params=pltpu.CompilerParams(
+            collective_id=0, has_side_effects=True, vmem_limit_bytes=VMEM_BYTES
+        ),
+    )(*(pltpu.with_memory_space_constraint(w, pltpu.HBM) for w in (wind_u, wind_v)))
     root = math.sqrt(2 * lat_size * cells * lon_size * width)
     return pl.pallas_call(
         functools.partial(finish, root),
@@ -366,6 +401,7 @@
         ),
         in_specs=[vmem, vmem, vmem],
         out_specs=(vmem, vmem),
+        compiler_params=pltpu.CompilerParams(vmem_limit_bytes=VMEM_BYTES),
     )(*held)
 
 

time: 28 us -> 25.3 us (0.904)
  Pallas kernels: 27.2 us -> 24.5 us
    pallas_call x1, Pallas kernels: 25.1 us -> 23.4 us  [shards(): pl.pallas_call(functools.partial(kernel, sizes), out_shape=(pltpu.VMEM((s...]
    pallas_call x1, Pallas kernels: 2.08 us -> 1.11 us  [shards(): pl.pallas_call(functools.partial(finish, root), out_shape=(jax.ShapeDtype...]
where the time goes in v3:
time: 25.3 us; the launch traced here: 25.1 us
  Pallas kernels  24.5 us (97%)
  between operations  0.64 us (3%)
    pallas_call x1, Pallas kernels, shards(): pl.pallas_call(functools.partial(kernel, sizes), out_shape=(pltpu.VMEM((s...  23.4 us
    pallas_call x1, Pallas kernels, shards(): pl.pallas_call(functools.partial(finish, root), out_shape=(jax.ShapeDtype...  1.11 us

profile of v3, /device:TPU:0, one launch (start us, length us, event | category | flops | bytes accessed | tf_op | source)
XLA Modules:
  0.0 25.1 jit_solution(14797587922298308864)
XLA Ops:
  0.6 23.4 %shard_map.41 = (f32[32,2048]{1,0:T(8,128)S(1)}, f32[32,128]{1,0:T(8,128)S(1)}, f32[32,128]{1,0:T(8,128)S(1)}) custom-call(f32[32,8,128]{2,1,0:T(8,128)} %u_hbm.1, f32[32,8,128]{2,1,0:T(8,128)} %v_hbm.1), custom_call_target="tpu_custom_call" | custom-call | tf_op jit(solution)/shard_map/pallas_call | solution.py:362
  24.0 1.1 %shard_map.42 = (f32[32,2,8,128]{3,2,1,0:T(8,128)}, f32[32,32]{1,0:T(8,128)}) custom-call(f32[32,2048]{1,0:T(8,128)S(1)} %get-tuple-element.5.solved_ref, f32[32,128]{1,0:T(8,128)S(1)} %get-tuple-element.6.first_ref, f32[32,128]{1,0:T(8,128)S(1)} %get-tuple-element.7.second_ref), custom_call_target="tpu_custom_call" | custom-call | tf_op jit(solution)/shard_map/pallas_call | solution.py:396

commit v4 on v3

--- a/solution.py
+++ b/solution.py
@@ -27,6 +27,21 @@
         precision=lax.Precision.HIGHEST,
         preferred_element_type=jnp.float32,
     )
+
+
+def two(tile):
+    high = tile.astype(jnp.bfloat16)
+    return high, (tile - high.astype(jnp.float32)).astype(jnp.bfloat16)
+
+
+def pair_dot(left, right, dims):
+    a, b = two(left)
+    x, y = two(right)
+
+    def one(m, n):
+        return lax.dot_general(m, n, (dims, ((), ())), preferred_element_type=jnp.float32)
+
+    return one(a, x) + (one(a, y) + one(b, x))
 
 
 def roll(tile, shift):
@@ -317,7 +332,7 @@
     gram = dot(block, block, ((1,), (1,)))
     first = factorize(merged(pack_gram(gram), 0), snaps)
     solved = dot(first[:, :snaps], block, ((1,), (0,)))
-    gram = dot(solved, solved, ((1,), (1,)))
+    gram = pair_dot(solved, solved, ((1,), (1,)))
     solved_ref[...] = solved
     first_ref[...] = first
     second_ref[...] = factorize(merged(pack_gram(gram), 1), snaps)
@@ -334,7 +349,7 @@
 def finish(root, solved_ref, first_ref, second_ref, modes_ref, factor_ref):
     snaps, _, cells, width = modes_ref.shape
     first, second = first_ref[...], second_ref[...]
-    modes = dot(second[:, :snaps] * root, solved_ref[...], ((1,), (0,)))
+    modes = pair_dot(second[:, :snaps] * root, solved_ref[...], ((1,), (0,)))
     for f in range(2):
         for i in range(cells):
             at = (f * cells + i) * width

time: 25.3 us -> 25.2 us (level)
  no operation moved by 1% of the time
where the time goes in v4:
time: 25.2 us; the launch traced here: 25 us
  Pallas kernels  24.4 us (97%)
  between operations  0.64 us (3%)
    pallas_call x1, Pallas kernels, shards(): pl.pallas_call(functools.partial(kernel, sizes), out_shape=(pltpu.VMEM((s...  23.3 us
    pallas_call x1, Pallas kernels, shards(): pl.pallas_call(functools.partial(finish, root), out_shape=(jax.ShapeDtype...  1.06 us

profile of v4, /device:TPU:0, one launch (start us, length us, event | category | flops | bytes accessed | tf_op | source)
XLA Modules:
  0.0 25.0 jit_solution(17761065395066929980)
XLA Ops:
  0.6 23.3 %shard_map.41 = (f32[32,2048]{1,0:T(8,128)S(1)}, f32[32,128]{1,0:T(8,128)S(1)}, f32[32,128]{1,0:T(8,128)S(1)}) custom-call(f32[32,8,128]{2,1,0:T(8,128)} %u_hbm.1, f32[32,8,128]{2,1,0:T(8,128)} %v_hbm.1), custom_call_target="tpu_custom_call" | custom-call | tf_op jit(solution)/shard_map/pallas_call | solution.py:377
  24.0 1.1 %shard_map.42 = (f32[32,2,8,128]{3,2,1,0:T(8,128)}, f32[32,32]{1,0:T(8,128)}) custom-call(f32[32,2048]{1,0:T(8,128)S(1)} %get-tuple-element.5.solved_ref, f32[32,128]{1,0:T(8,128)S(1)} %get-tuple-element.6.first_ref, f32[32,128]{1,0:T(8,128)S(1)} %get-tuple-element.7.second_ref), custom_call_target="tpu_custom_call" | custom-call | tf_op jit(solution)/shard_map/pallas_call | solution.py:411
